TPU v7x, 256 devices: a whole 4x4x8 slice. The times are simulated.
256 devices in a mesh: seq: 16 (over z, core), head: 16 (over x, y).
Axes of the slice: x: 4, y: 4, z: 8, core: 2. Of those that a mesh axis runs over, the one named last changes fastest.
Arguments:
- x_in: bfloat16 [16384, 8192], P('seq', 'head'), may hold values from -6 to 6
- z_gate: bfloat16 [16384, 8192], P('seq', 'head'), may hold values from -6 to 6
- b_in: bfloat16 [16384, 128], P('seq'), may hold values from -6.5 to 6.5
- c_in: bfloat16 [16384, 128], P('seq'), may hold values from -6 to 6
- dt_raw: float32 [16384, 128], P('seq', 'head'), may hold values from -7.5 to 263.144
- a_log: float32 [128], P('head'), may hold values from -12 to 3.5, as said below
- d_skip: float32 [128], P('head'), may hold values from 0.5 to 1.5
- conv_x: float32 [4, 8192], P(None, 'head'), may hold values from -3 to 3
- conv_bc: float32 [4, 256], replicated, may hold values from -0.8 to 0.8
- norm_gain: float32 [8192], P('head'), may hold values from 0.1 to 1.9
- w_out: bfloat16 [8192, 4096], P('head'), may hold values from -0.0625 to 0.0625
Outputs:
- mixed: bfloat16 [16384, 4096], P(('seq', 'head'))
Inputs may be any that keep to these rules, and one draw needn't show every extreme that they name: `a_log`: logarithm of each head's decay rate.
All inputs are finite; a program needn't handle non-finite values.
Results may differ from a plain program's by a relative error of at most 0.018.
Values may be sent and summed in bfloat16 or wider, within the bound.
No kernel may reach another device: no remote copies, remote signals or barrier semaphores. Data moves between devices by JAX's collectives and lax.ppermute only.
A program may use at most 64 MiB of HBM per device.

v0:
```python
import jax
import jax.numpy as jnp
from jax import lax
from jax.sharding import PartitionSpec as P

HEAD_DIM = 64
SPAN = 256
INNER = 8192
norm_eps = 1e-05


def passed_along(block, axis, distance):
    devices = range(lax.axis_size(axis))
    route = [(i - distance, i) for i in devices if i - distance in devices]
    return lax.ppermute(block, axis, route)


def carried_in(x, axis, combine, identity):
    devices, here = (lax.axis_size(axis), lax.axis_index(axis))
    everything = jax.tree.map(
        lambda part, kind: lax.all_gather(part.astype(kind), axis), x, (jnp.bfloat16, jnp.bfloat16)
    )
    start = jax.tree.map(
        lambda part, zero: jnp.broadcast_to(jnp.asarray(zero, part.dtype), part.shape), x, identity
    )

    def turn(k, before):
        reached = k < here
        new = combine(
            before, jax.tree.map(lambda part, own: part[k].astype(own.dtype), everything, x)
        )
        return jax.tree.map(lambda a, b: jnp.where(reached, a, b), new, before)

    return lax.fori_loop(0, devices, turn, start)


def causal_conv(values, rim, weight):
    n_rows = values.shape[0]
    padded = jnp.concatenate([rim.astype(jnp.float32), values.astype(jnp.float32)], axis=0)
    result = weight[0][None, :] * padded[0:n_rows]
    for offset in range(1, weight.shape[0]):
        result = result + weight[offset][None, :] * padded[offset : offset + n_rows]
    return jax.nn.silu(result).astype(jnp.bfloat16)


def span_step(memory, pieces):
    x_part, b_part, c_part, step_part, decay_part = pieces
    running = jnp.cumsum(decay_part, axis=0)
    length = x_part.shape[0]
    positions = lax.iota(jnp.int32, length)
    causal = positions[:, None] >= positions[None, :]
    spread = jnp.where(causal[:, :, None], running[:, None, :] - running[None, :, :], -1e30)
    scores = jnp.dot(c_part, b_part.T, preferred_element_type=jnp.float32)
    b_wide = b_part.astype(jnp.float32)
    c_wide = c_part.astype(jnp.float32)
    mixing = jnp.exp(spread) * scores[:, :, None] * step_part[None, :, :]
    inside = jnp.einsum("ijh,jhp->ihp", mixing, x_part, precision=lax.Precision.HIGHEST)
    earlier = (
        jnp.einsum("in,hpn->ihp", c_wide, memory, precision=lax.Precision.HIGHEST)
        * jnp.exp(running)[:, :, None]
    )
    final_decay = running[length - 1]
    weights = jnp.exp(final_decay[None, :] - running) * step_part
    update = jnp.einsum(
        "jhp,jn->hpn", x_part * weights[:, :, None], b_wide, precision=lax.Precision.HIGHEST
    )
    new_memory = memory * jnp.exp(final_decay)[:, None, None] + update
    return (new_memory, inside + earlier)


def local(x_in, z_gate, b_in, c_in, dt_raw, a_log, d_skip, conv_x, conv_bc, norm_gain, w_out):
    n_rows = x_in.shape[0]
    rim_rows = conv_x.shape[0] - 1
    state_size = b_in.shape[1]
    head_count = dt_raw.shape[1]
    bc_in = jnp.concatenate([b_in, c_in], axis=1)
    x_rim, bc_rim = passed_along((x_in[n_rows - rim_rows :], bc_in[n_rows - rim_rows :]), "seq", 1)
    x_conv = causal_conv(x_in, x_rim, conv_x)
    bc_conv = causal_conv(bc_in, bc_rim, conv_bc)
    b_conv = bc_conv[:, :state_size]
    c_conv = bc_conv[:, state_size:]
    dt_step = jax.nn.softplus(dt_raw)
    log_decay = -jnp.exp(a_log)[None, :] * dt_step
    x_heads = x_conv.astype(jnp.float32).reshape(n_rows, head_count, HEAD_DIM)
    blocks = n_rows // SPAN

    def split_blocks(values):
        return values.reshape((blocks, SPAN) + values.shape[1:])

    start = jnp.zeros((head_count, HEAD_DIM, state_size), jnp.float32)
    final_state, outputs = lax.scan(
        span_step,
        start,
        (
            split_blocks(x_heads),
            split_blocks(b_conv),
            split_blocks(c_conv),
            split_blocks(dt_step),
            split_blocks(log_decay),
        ),
    )
    total_decay = jnp.sum(log_decay, axis=0)

    def combine(earlier, later):
        return (earlier[0] + later[0], jnp.exp(later[0])[:, None, None] * earlier[1] + later[1])

    identity = (jnp.zeros_like(total_decay), jnp.zeros_like(final_state))
    _, incoming = carried_in((total_decay, final_state), "seq", combine, identity)
    inside_segment = jnp.cumsum(log_decay, axis=0)
    carried = (
        jnp.einsum(
            "ln,hpn->lhp", c_conv.astype(jnp.float32), incoming, precision=lax.Precision.HIGHEST
        )
        * jnp.exp(inside_segment)[:, :, None]
    )
    ssd = outputs.reshape(n_rows, head_count, HEAD_DIM) + carried + d_skip[None, :, None] * x_heads
    gated = ssd.reshape(n_rows, head_count * HEAD_DIM) * jax.nn.silu(z_gate.astype(jnp.float32))
    squares = lax.psum(jnp.sum(gated * gated, axis=1), "head")
    normed = (gated * lax.rsqrt(squares / INNER + norm_eps)[:, None] * norm_gain[None, :]).astype(
        jnp.bfloat16
    )
    return lax.psum_scatter(
        jnp.dot(normed, w_out, preferred_element_type=jnp.float32).astype(jnp.bfloat16),
        "head",
        scatter_dimension=0,
        tiled=True,
    )


def solution(mesh):
    in_specs = (
        P("seq", "head"),
        P("seq", "head"),
        P("seq", None),
        P("seq", None),
        P("seq", "head"),
        P("head"),
        P("head"),
        P(None, "head"),
        P(),
        P("head"),
        P("head", None),
    )
    out_specs = P(("seq", "head"), None)
    return jax.shard_map(local, mesh=mesh, in_specs=in_specs, out_specs=out_specs, check_vma=False)
```

profile of v0, /device:TPU:2, one launch (start us, length us, event | category | flops | bytes accessed | tf_op | source)
XLA Modules:
  0.0 321.9 jit_solution(4716732184914080873)
XLA Ops:
  6.5 1.1 constant_dynamic-update-slice_fusion.1
  7.6 1.0 constant_dynamic-update-slice_fusion
  8.7 1.7 collective-permute-start.1
  10.4 0.7 slice.70
  11.1 4.1 %collective-permute-start = (bf16[3,512]{1,0:T(4,128)(2,1)S(1)}, bf16[3,512]{1,0:T(4,128)(2,1)S(1)}, u32[]{:S(2)}, u32[]{:S(2)}) collective-permute-start(bf16[3,512]{1,0:T(4,128)(2,1)S(1)} %slice.70), channel_id=1, source_target_pairs={{0,16},{16,32},{32,48},{48,64},{64,80},{80,96},{96,112},{112,128},... | collective-permute-start | bytes 9224 | tf_op jit(solution)/shard_map/ppermute | solution.py:15
  15.2 0.9 fusion.72
  16.7 0.9 fusion.70
  17.7 0.8 fusion.73
  18.6 1.6 convert_element_type.72
  20.9 0.8 fusion.71
  21.9 1.3 fusion.64
  23.1 2.4 reshape.114
  25.5 3.8 %copy.35 = f32[4,256,8,64]{1,3,2,0:T(8,128)} copy(f32[4,256,8,64]{3,2,1,0:T(8,128)} %reshape.114) | data formatting | bytes 4194304
  29.3 85.7 %while.27 = (s32[]{:T(128)}, f32[8,64,128]{2,1,0:T(8,128)S(1)}, f32[4,256,8,64]{1,0,3,2:T(4,128)}, f32[4,256,8]{1,2,0:T(8,128)S(1)}, f32[4,256,8,64]{1,3,2,0:T(8...) while((s32[]{:T(128)}, f32[8,64,128]{2,1,0:T(8,128)S(1)}, ...), condition=%wide.region_3.4_spmd.clone, body=%wide.region_0.3_spmd.clone.sunk | while | flops 825167872 | bytes 6557484 | solution.py:91
  30.5 1.1 fusion.98
  31.6 3.5 %fusion.99 = f32[256,8,64]{0,2,1:T(8,128)S(1)} fusion(f32[256,8]{0,1:T(8,128)S(1)} %get-tuple-element.338, f32[256,256]{1,0:T(8,128)S(1)} %fusion.98, f32[256,8]{0,1:T(8,128)S(1)} %get-tuple-element.336, pred[256,256]{1,0:T(8,128)(4,1)S(1)} %iota_compare_fusion.2, f32[4,256,8,64]{1,3,2,0:T(8,128)} %get-tuple-element.371, s32[]{:T(128)} %get-tuple-element.356), kind=kOutput, calls=%fused_computation.12.clone.1 | convolution fusion | flops 404750336 | bytes 1401344 | tf_op jit(solution)/shard_map/while/body/eval_jaxpr/ijh,jhp->ihp/dot_general | solution.py:57
  35.1 1.2 fusion.100
  36.9 12.3 %dynamic_update_slice.6 = f32[4,256,8,64]{1,0,3,2:T(4,128)} dynamic-update-slice(f32[4,256,8,64]{1,0,3,2:T(4,128)} %get-tuple-element.358, f32[1,256,8,64]{1,0,3,2:T(1,128)S(1)} %copy.52, s32[]{:T(128)} %get-tuple-element.356, s32[]{:T(128)} %constant.63.clone.1..sunk, s32[]{:T(128)} %constant.63.clone.1..sunk, s32[]{:T(128)} %constant.63.clone.1..sunk) | dynamic-update-slice | bytes 1048580 | tf_op jit(solution)/shard_map/while/body/jit(dynamic_update_index_in_dim)/dynamic_update_slice | solution.py:91
  49.2 1.5 convolution_add_fusion.2
  51.9 1.1 fusion.98
  53.0 3.5 %fusion.99 = f32[256,8,64]{0,2,1:T(8,128)S(1)} fusion(f32[256,8]{0,1:T(8,128)S(1)} %get-tuple-element.338, f32[256,256]{1,0:T(8,128)S(1)} %fusion.98, f32[256,8]{0,1:T(8,128)S(1)} %get-tuple-element.336, pred[256,256]{1,0:T(8,128)(4,1)S(1)} %iota_compare_fusion.2, f32[4,256,8,64]{1,3,2,0:T(8,128)} %get-tuple-element.371, s32[]{:T(128)} %get-tuple-element.356), kind=kOutput, calls=%fused_computation.12.clone.1 | convolution fusion | flops 404750336 | bytes 1401344 | tf_op jit(solution)/shard_map/while/body/eval_jaxpr/ijh,jhp->ihp/dot_general | solution.py:57
  56.5 1.2 fusion.100
  58.3 12.3 %dynamic_update_slice.6 = f32[4,256,8,64]{1,0,3,2:T(4,128)} dynamic-update-slice(f32[4,256,8,64]{1,0,3,2:T(4,128)} %get-tuple-element.358, f32[1,256,8,64]{1,0,3,2:T(1,128)S(1)} %copy.52, s32[]{:T(128)} %get-tuple-element.356, s32[]{:T(128)} %constant.63.clone.1..sunk, s32[]{:T(128)} %constant.63.clone.1..sunk, s32[]{:T(128)} %constant.63.clone.1..sunk) | dynamic-update-slice | bytes 1048580 | tf_op jit(solution)/shard_map/while/body/jit(dynamic_update_index_in_dim)/dynamic_update_slice | solution.py:91
  70.6 1.5 convolution_add_fusion.2
  73.3 1.1 fusion.98
  74.4 3.5 %fusion.99 = f32[256,8,64]{0,2,1:T(8,128)S(1)} fusion(f32[256,8]{0,1:T(8,128)S(1)} %get-tuple-element.338, f32[256,256]{1,0:T(8,128)S(1)} %fusion.98, f32[256,8]{0,1:T(8,128)S(1)} %get-tuple-element.336, pred[256,256]{1,0:T(8,128)(4,1)S(1)} %iota_compare_fusion.2, f32[4,256,8,64]{1,3,2,0:T(8,128)} %get-tuple-element.371, s32[]{:T(128)} %get-tuple-element.356), kind=kOutput, calls=%fused_computation.12.clone.1 | convolution fusion | flops 404750336 | bytes 1401344 | tf_op jit(solution)/shard_map/while/body/eval_jaxpr/ijh,jhp->ihp/dot_general | solution.py:57
  78.0 1.2 fusion.100
  79.7 12.3 %dynamic_update_slice.6 = f32[4,256,8,64]{1,0,3,2:T(4,128)} dynamic-update-slice(f32[4,256,8,64]{1,0,3,2:T(4,128)} %get-tuple-element.358, f32[1,256,8,64]{1,0,3,2:T(1,128)S(1)} %copy.52, s32[]{:T(128)} %get-tuple-element.356, s32[]{:T(128)} %constant.63.clone.1..sunk, s32[]{:T(128)} %constant.63.clone.1..sunk, s32[]{:T(128)} %constant.63.clone.1..sunk) | dynamic-update-slice | bytes 1048580 | tf_op jit(solution)/shard_map/while/body/jit(dynamic_update_index_in_dim)/dynamic_update_slice | solution.py:91
  92.1 1.5 convolution_add_fusion.2
  94.7 1.1 fusion.98
  95.8 3.5 %fusion.99 = f32[256,8,64]{0,2,1:T(8,128)S(1)} fusion(f32[256,8]{0,1:T(8,128)S(1)} %get-tuple-element.338, f32[256,256]{1,0:T(8,128)S(1)} %fusion.98, f32[256,8]{0,1:T(8,128)S(1)} %get-tuple-element.336, pred[256,256]{1,0:T(8,128)(4,1)S(1)} %iota_compare_fusion.2, f32[4,256,8,64]{1,3,2,0:T(8,128)} %get-tuple-element.371, s32[]{:T(128)} %get-tuple-element.356), kind=kOutput, calls=%fused_computation.12.clone.1 | convolution fusion | flops 404750336 | bytes 1401344 | tf_op jit(solution)/shard_map/while/body/eval_jaxpr/ijh,jhp->ihp/dot_general | solution.py:57
  99.4 1.2 fusion.100
  101.2 12.3 %dynamic_update_slice.6 = f32[4,256,8,64]{1,0,3,2:T(4,128)} dynamic-update-slice(f32[4,256,8,64]{1,0,3,2:T(4,128)} %get-tuple-element.358, f32[1,256,8,64]{1,0,3,2:T(1,128)S(1)} %copy.52, s32[]{:T(128)} %get-tuple-element.356, s32[]{:T(128)} %constant.63.clone.1..sunk, s32[]{:T(128)} %constant.63.clone.1..sunk, s32[]{:T(128)} %constant.63.clone.1..sunk) | dynamic-update-slice | bytes 1048580 | tf_op jit(solution)/shard_map/while/body/jit(dynamic_update_index_in_dim)/dynamic_update_slice | solution.py:91
  113.5 1.5 convolution_add_fusion.2
  115.0 0.7 convert_element_type.80
  117.4 26.1 %all-reduce = bf16[128]{0:T(256)(128)(2,1)S(1)} all-reduce(bf16[128]{0:T(256)(128)(2,1)S(1)} %dynamic-update-slice), channel_id=2, replica_groups=mesh['seq'=16,'head'=16] {'seq'}, use_global_device_ids=true, to_apply=%add | all-reduce | flops 128 | bytes 512
  143.6 2.3 reduce-window.16
  146.3 1.8 copy.38
  148.1 2.4 reshape.95
  150.5 6.7 %all-gather.4.cloned.1.call-done = bf16[128,64,128]{2,1,0:T(8,128)(2,1)} async-done(((bf16[8,64,128]{2,1,0:T(8,128)(2,1)}), bf16[128,64,128]{2,1,0:T(8,128)(2,1)}) %all-gather.4.cloned.1.call-update) | async-done | bytes 2097168 | tf_op jit(solution)/shard_map/all_gather | solution.py:21
  157.2 16.9 %while.28 = (s32[]{:T(128)}, f32[8,64,128]{2,1,0:T(8,128)S(1)}, s32[]{:T(128)}, bf16[16,8]{1,0:T(8,128)(2,1)S(1)}, bf16[16,8,64,128]{3,2,1,0:T(8,128)(2,1)}, /*index=5*/s32[]{:T(128)}, s32[]{:T(128)}) while((s32[]{:T(128)}, f32[8,64,128]{2,1,0:T(8,128)S(1)}, s32[]{:T(128)}, bf16[16,8]{1,0:T(8,128)(2,1)S(1)}, ...), condition=%wide.region_6.7_spmd.clone, body=%wide.region_5.6_spmd.clone.sunk | while | flops 327692 | bytes 655545 | solution.py:34
  157.2 1.0 fusion.101
  158.3 1.0 fusion.101
  159.3 1.0 fusion.101
  160.4 1.0 fusion.101
  161.4 1.0 fusion.101
  162.5 1.0 fusion.101
  163.5 1.0 fusion.101
  164.6 1.0 fusion.101
  165.7 1.0 fusion.101
  166.7 1.0 fusion.101
  167.8 1.0 fusion.101
  168.8 1.0 fusion.101
  169.9 1.0 fusion.101
  170.9 1.0 fusion.101
  172.0 1.0 fusion.101
  173.0 1.0 fusion.101
  174.1 1.0 fusion.65
  175.7 2.1 multiply_add_fusion
  177.8 2.0 copy.39
  179.8 0.7 multiply_reduce_fusion
  180.5 34.3 %psum.7 = f32[1024]{0:T(1024)S(1)} all-reduce(f32[1024]{0:T(1024)S(1)} %multiply_reduce_fusion), channel_id=1, replica_groups=mesh['seq'=16,'head'=16] {'head'}, use_global_device_ids=true, to_apply=%region_10.11 | all-reduce | flops 1024 | bytes 8192 | tf_op jit(solution)/shard_map/psum | solution.py:118
  214.8 9.5 %convolution_convert_fusion = bf16[1024,4096]{1,0:T(8,128)(2,1)} fusion(bf16[512,4096]{1,0:T(8,128)(2,1)} %param.25, f32[512]{0:T(512)S(1)} %copy-done.5, f32[1024]{0:T(1024)S(1)} %add_rsqrt_fusion, f32[1024,512]{1,0:T(8,128)S(1)} %copy.39, bf16[1024,512]{1,0:T(8,128)(2,1)S(1)} %copy-done.3), kind=kOutput, calls=%fused_computation.51 | convolution fusion | flops 4303880192 | bytes 15734784 | tf_op jit(solution)/shard_map/dot_general | solution.py:123
  224.3 90.8 %reduce-scatter.2.cloned.1.call-done = bf16[64,4096]{1,0:T(8,128)(2,1)} async-done(((bf16[1024,4096]{1,0:T(8,128)(2,1)}), bf16[64,4096]{1,0:T(8,128)(2,1)}) %reduce-scatter.2.cloned.1.call-update) | async-done | bytes 524304 | tf_op jit(solution)/shard_map/reduce_scatter | solution.py:122
  (99 shorter events, 10.6 us)
Async XLA Ops:
  6.5 12.1 %copy-start.2 = (bf16[1024,512]{1,0:T(8,128)(2,1)S(1)}, bf16[1024,512]{1,0:T(8,128)(2,1)}, u32[]{:S(2)}) copy-start(bf16[1024,512]{1,0:T(8,128)(2,1)} %param.15) | copy-start | bytes 3145732
  6.5 150.7 %all-gather.4.cloned.1.call-start = ((), (), s32[]{:S(2)}) async-start(), calls=%async_computation.2 | async-start | bytes 2228224 | tf_op jit(solution)/shard_map/all_gather | solution.py:21
  8.7 11.6 %collective-permute-start.1 = (bf16[3,256]{1,0:T(4,128)(2,1)S(1)}, bf16[3,256]{1,0:T(4,128)(2,1)S(1)}, u32[]{:S(2)}, u32[]{:S(2)}) collective-permute-start(bf16[3,256]{1,0:T(4,128)(2,1)S(1)} %slice.98), channel_id=1, source_target_pairs={{0,16},{16,32},{32,48},{48,64},{64,80},{80,96},{96,112},{112,128},... | collective-permute-start | bytes 4616 | tf_op jit(solution)/shard_map/ppermute | solution.py:15
  11.1 10.6 %collective-permute-start = (bf16[3,512]{1,0:T(4,128)(2,1)S(1)}, bf16[3,512]{1,0:T(4,128)(2,1)S(1)}, u32[]{:S(2)}, u32[]{:S(2)}) collective-permute-start(bf16[3,512]{1,0:T(4,128)(2,1)S(1)} %slice.70), channel_id=1, source_target_pairs={{0,16},{16,32},{32,48},{48,64},{64,80},{80,96},{96,112},{112,128},... | collective-permute-start | bytes 9224 | tf_op jit(solution)/shard_map/ppermute | solution.py:15
  20.3 1.6 copy-start
  29.3 86.5 %copy-start.6 = (u32[256]{0:T(256)S(1)}, u32[256]{0:T(256)}, u32[]{:S(2)}) copy-start(u32[256]{0:T(256)} %constant.75) | copy-start | bytes 3076
  115.7 199.3 %reduce-scatter.2.cloned.1.call-start = ((), (), s32[]{:S(2)}) async-start(), calls=%async_computation.1 | async-start | bytes 8912896 | tf_op jit(solution)/shard_map/reduce_scatter | solution.py:122
  174.1 1.6 copy-start.1
  174.1 1.6 copy-start.4
  177.8 2.0 copy-start.3
  179.8 35.0 %copy-start.5 = (f32[512]{0:T(512)S(1)}, f32[512]{0:T(512)}, u32[]{:S(2)}) copy-start(f32[512]{0:T(512)} %param.24) | copy-start | bytes 6148
Sparse Core Ops, SparseCore 0:
  115.8 41.3 all-gather.3
  224.4 90.5 reduce-scatter.1
where the time goes:
time: 324 us; the launch traced here: 322 us
  waiting for transfers between devices  97.5 us (30%)
  local copies, waits for them, and re-layouts  72.5 us (22%)
  blocking collectives  60.3 us (19%)
  matrix products  39.8 us (12%)
  other arithmetic  30.9 us (10%)
  between operations  14.3 us (4%)
  starting transfers between devices  5.88 us (2%)
    reduce_scatter x1, waiting for transfers between devices, local(): lax.psum_scatter(jnp.dot(normed, w_out, preferred_element_type=jnp.float3...  90.8 us
    dynamic_update_slice x8, local copies, waits for them, and re-layouts, local(): lax.scan(span_step, start, (split_blocks(x_heads), split_blocks(b_conv),...  51.4 us
    psum x1, blocking collectives, local(): squares = lax.psum(jnp.sum(gated * gated, axis=1), 'head')  34.3 us
    unnamed x1, blocking collectives  26.1 us
    select_n x16, other arithmetic, turn(): return jax.tree.map(lambda a, b: jnp.where(reached, a, b), new, before)  16.2 us
    dot_general x4, matrix products, span_step(): jnp.einsum('ijh,jhp->ihp', mixing, x_part, precision=lax.Precision.HIGHEST)  14.2 us
    dot_general x1, matrix products, local(): jnp.dot(normed, w_out, preferred_element_type=jnp.float32)  9.45 us
    all_gather x1, waiting for transfers between devices, carried_in(): lax.all_gather(part.astype(kind), axis)  6.71 us
  transfers between devices with their start and end apart: 4, of which 2 were waited for; matrix products, arithmetic and copies ran while one was open for 5% of the time, Pallas kernels for 0%

commit v1 on v0

--- a/solution.py
+++ b/solution.py
@@ -115,7 +115,7 @@
     )
     ssd = outputs.reshape(n_rows, head_count, HEAD_DIM) + carried + d_skip[None, :, None] * x_heads
     gated = ssd.reshape(n_rows, head_count * HEAD_DIM) * jax.nn.silu(z_gate.astype(jnp.float32))
-    squares = lax.psum(jnp.sum(gated * gated, axis=1), "head")
+    squares = jnp.sum(lax.all_gather(jnp.sum(gated * gated, axis=1), "head"), axis=0)
     normed = (gated * lax.rsqrt(squares / INNER + norm_eps)[:, None] * norm_gain[None, :]).astype(
         jnp.bfloat16
     )

time: 324 us -> 313 us (0.966)
  blocking collectives: 60.3 us -> 49.7 us
    psum x1 -> x0, blocking collectives: 34.3 us -> none  [local(): squares = lax.psum(jnp.sum(gated * gated, axis=1), 'head')]
    all_gather x0 -> x1, blocking collectives: none -> 23.6 us  [local(): lax.all_gather(jnp.sum(gated * gated, axis=1), 'head')]
    unnamed x20 -> x18, local copies, waits for them, and re-layouts: 6.53 us -> 6.53 us
where the time goes in v1:
time: 313 us; the launch traced here: 310 us
  waiting for transfers between devices  94.3 us (30%)
  local copies, waits for them, and re-layouts  72.4 us (23%)
  blocking collectives  49.7 us (16%)
  matrix products  41 us (13%)
  other arithmetic  32.1 us (10%)
  between operations  14.3 us (5%)
  starting transfers between devices  5.88 us (2%)
    reduce_scatter x1, waiting for transfers between devices, local(): lax.psum_scatter(jnp.dot(normed, w_out, preferred_element_type=jnp.float3...  87.6 us
    dynamic_update_slice x8, local copies, waits for them, and re-layouts, local(): lax.scan(span_step, start, (split_blocks(x_heads), split_blocks(b_conv),...  51.4 us
    unnamed x1, blocking collectives  26.1 us
    all_gather x1, blocking collectives, local(): lax.all_gather(jnp.sum(gated * gated, axis=1), 'head')  23.6 us
    select_n x16, other arithmetic, turn(): return jax.tree.map(lambda a, b: jnp.where(reached, a, b), new, before)  16.2 us
    dot_general x4, matrix products, span_step(): jnp.einsum('ijh,jhp->ihp', mixing, x_part, precision=lax.Precision.HIGHEST)  14.2 us
    dot_general x1, matrix products, local(): jnp.dot(normed, w_out, preferred_element_type=jnp.float32)  10.7 us
    all_gather x1, waiting for transfers between devices, carried_in(): lax.all_gather(part.astype(kind), axis)  6.71 us
  transfers between devices with their start and end apart: 4, of which 2 were waited for; matrix products, arithmetic and copies ran while one was open for 5% of the time, Pallas kernels for 0%

profile of v1, /device:TPU:2, one launch (start us, length us, event | category | flops | bytes accessed | tf_op | source)
XLA Modules:
  0.0 310.4 jit_solution(18087415153896727078)
XLA Ops:
  6.5 1.1 constant_dynamic-update-slice_fusion.1
  7.6 1.0 constant_dynamic-update-slice_fusion
  8.7 1.7 collective-permute-start.1
  10.4 0.7 slice.70
  11.1 4.1 %collective-permute-start = (bf16[3,512]{1,0:T(4,128)(2,1)S(1)}, bf16[3,512]{1,0:T(4,128)(2,1)S(1)}, u32[]{:S(2)}, u32[]{:S(2)}) collective-permute-start(bf16[3,512]{1,0:T(4,128)(2,1)S(1)} %slice.70), channel_id=1, source_target_pairs={{0,16},{16,32},{32,48},{48,64},{64,80},{80,96},{96,112},{112,128},... | collective-permute-start | bytes 9224 | tf_op jit(solution)/shard_map/ppermute | solution.py:15
  15.2 0.9 fusion.72
  16.7 0.9 fusion.70
  17.7 0.8 fusion.73
  18.6 1.6 convert_element_type.72
  20.9 0.8 fusion.71
  21.9 1.3 fusion.64
  23.1 2.4 reshape.119
  25.5 3.8 %copy.41 = f32[4,256,8,64]{1,3,2,0:T(8,128)} copy(f32[4,256,8,64]{3,2,1,0:T(8,128)} %reshape.119) | data formatting | bytes 4194304
  29.3 85.7 %while.27 = (s32[]{:T(128)}, f32[8,64,128]{2,1,0:T(8,128)S(1)}, f32[4,256,8,64]{1,0,3,2:T(4,128)}, f32[4,256,8]{1,2,0:T(8,128)S(1)}, f32[4,256,8,64]{1,3,2,0:T(8...) while((s32[]{:T(128)}, f32[8,64,128]{2,1,0:T(8,128)S(1)}, ...), condition=%wide.region_3.4_spmd.clone, body=%wide.region_0.3_spmd.clone.sunk | while | flops 825167872 | bytes 6557484 | solution.py:91
  30.5 1.1 fusion.98
  31.6 3.5 %fusion.99 = f32[256,8,64]{0,2,1:T(8,128)S(1)} fusion(f32[256,8]{0,1:T(8,128)S(1)} %get-tuple-element.346, f32[256,256]{1,0:T(8,128)S(1)} %fusion.98, f32[256,8]{0,1:T(8,128)S(1)} %get-tuple-element.344, pred[256,256]{1,0:T(8,128)(4,1)S(1)} %iota_compare_fusion.2, f32[4,256,8,64]{1,3,2,0:T(8,128)} %get-tuple-element.379, s32[]{:T(128)} %get-tuple-element.364), kind=kOutput, calls=%fused_computation.12.clone.1 | convolution fusion | flops 404750336 | bytes 1401344 | tf_op jit(solution)/shard_map/while/body/eval_jaxpr/ijh,jhp->ihp/dot_general | solution.py:57
  35.1 1.2 fusion.100
  36.9 12.3 %dynamic_update_slice.6 = f32[4,256,8,64]{1,0,3,2:T(4,128)} dynamic-update-slice(f32[4,256,8,64]{1,0,3,2:T(4,128)} %get-tuple-element.366, f32[1,256,8,64]{1,0,3,2:T(1,128)S(1)} %copy.59, s32[]{:T(128)} %get-tuple-element.364, s32[]{:T(128)} %constant.63.clone.1..sunk, s32[]{:T(128)} %constant.63.clone.1..sunk, s32[]{:T(128)} %constant.63.clone.1..sunk) | dynamic-update-slice | bytes 1048580 | tf_op jit(solution)/shard_map/while/body/jit(dynamic_update_index_in_dim)/dynamic_update_slice | solution.py:91
  49.2 1.5 convolution_add_fusion.2
  51.9 1.1 fusion.98
  53.0 3.5 %fusion.99 = f32[256,8,64]{0,2,1:T(8,128)S(1)} fusion(f32[256,8]{0,1:T(8,128)S(1)} %get-tuple-element.346, f32[256,256]{1,0:T(8,128)S(1)} %fusion.98, f32[256,8]{0,1:T(8,128)S(1)} %get-tuple-element.344, pred[256,256]{1,0:T(8,128)(4,1)S(1)} %iota_compare_fusion.2, f32[4,256,8,64]{1,3,2,0:T(8,128)} %get-tuple-element.379, s32[]{:T(128)} %get-tuple-element.364), kind=kOutput, calls=%fused_computation.12.clone.1 | convolution fusion | flops 404750336 | bytes 1401344 | tf_op jit(solution)/shard_map/while/body/eval_jaxpr/ijh,jhp->ihp/dot_general | solution.py:57
  56.5 1.2 fusion.100
  58.3 12.3 %dynamic_update_slice.6 = f32[4,256,8,64]{1,0,3,2:T(4,128)} dynamic-update-slice(f32[4,256,8,64]{1,0,3,2:T(4,128)} %get-tuple-element.366, f32[1,256,8,64]{1,0,3,2:T(1,128)S(1)} %copy.59, s32[]{:T(128)} %get-tuple-element.364, s32[]{:T(128)} %constant.63.clone.1..sunk, s32[]{:T(128)} %constant.63.clone.1..sunk, s32[]{:T(128)} %constant.63.clone.1..sunk) | dynamic-update-slice | bytes 1048580 | tf_op jit(solution)/shard_map/while/body/jit(dynamic_update_index_in_dim)/dynamic_update_slice | solution.py:91
  70.6 1.5 convolution_add_fusion.2
  73.3 1.1 fusion.98
  74.4 3.5 %fusion.99 = f32[256,8,64]{0,2,1:T(8,128)S(1)} fusion(f32[256,8]{0,1:T(8,128)S(1)} %get-tuple-element.346, f32[256,256]{1,0:T(8,128)S(1)} %fusion.98, f32[256,8]{0,1:T(8,128)S(1)} %get-tuple-element.344, pred[256,256]{1,0:T(8,128)(4,1)S(1)} %iota_compare_fusion.2, f32[4,256,8,64]{1,3,2,0:T(8,128)} %get-tuple-element.379, s32[]{:T(128)} %get-tuple-element.364), kind=kOutput, calls=%fused_computation.12.clone.1 | convolution fusion | flops 404750336 | bytes 1401344 | tf_op jit(solution)/shard_map/while/body/eval_jaxpr/ijh,jhp->ihp/dot_general | solution.py:57
  78.0 1.2 fusion.100
  79.7 12.3 %dynamic_update_slice.6 = f32[4,256,8,64]{1,0,3,2:T(4,128)} dynamic-update-slice(f32[4,256,8,64]{1,0,3,2:T(4,128)} %get-tuple-element.366, f32[1,256,8,64]{1,0,3,2:T(1,128)S(1)} %copy.59, s32[]{:T(128)} %get-tuple-element.364, s32[]{:T(128)} %constant.63.clone.1..sunk, s32[]{:T(128)} %constant.63.clone.1..sunk, s32[]{:T(128)} %constant.63.clone.1..sunk) | dynamic-update-slice | bytes 1048580 | tf_op jit(solution)/shard_map/while/body/jit(dynamic_update_index_in_dim)/dynamic_update_slice | solution.py:91
  92.1 1.5 convolution_add_fusion.2
  94.7 1.1 fusion.98
  95.8 3.5 %fusion.99 = f32[256,8,64]{0,2,1:T(8,128)S(1)} fusion(f32[256,8]{0,1:T(8,128)S(1)} %get-tuple-element.346, f32[256,256]{1,0:T(8,128)S(1)} %fusion.98, f32[256,8]{0,1:T(8,128)S(1)} %get-tuple-element.344, pred[256,256]{1,0:T(8,128)(4,1)S(1)} %iota_compare_fusion.2, f32[4,256,8,64]{1,3,2,0:T(8,128)} %get-tuple-element.379, s32[]{:T(128)} %get-tuple-element.364), kind=kOutput, calls=%fused_computation.12.clone.1 | convolution fusion | flops 404750336 | bytes 1401344 | tf_op jit(solution)/shard_map/while/body/eval_jaxpr/ijh,jhp->ihp/dot_general | solution.py:57
  99.4 1.2 fusion.100
  101.2 12.3 %dynamic_update_slice.6 = f32[4,256,8,64]{1,0,3,2:T(4,128)} dynamic-update-slice(f32[4,256,8,64]{1,0,3,2:T(4,128)} %get-tuple-element.366, f32[1,256,8,64]{1,0,3,2:T(1,128)S(1)} %copy.59, s32[]{:T(128)} %get-tuple-element.364, s32[]{:T(128)} %constant.63.clone.1..sunk, s32[]{:T(128)} %constant.63.clone.1..sunk, s32[]{:T(128)} %constant.63.clone.1..sunk) | dynamic-update-slice | bytes 1048580 | tf_op jit(solution)/shard_map/while/body/jit(dynamic_update_index_in_dim)/dynamic_update_slice | solution.py:91
  113.5 1.5 convolution_add_fusion.2
  115.0 0.7 convert_element_type.80
  117.4 26.1 %all-reduce = bf16[128]{0:T(256)(128)(2,1)S(1)} all-reduce(bf16[128]{0:T(256)(128)(2,1)S(1)} %dynamic-update-slice), channel_id=2, replica_groups=mesh['seq'=16,'head'=16] {'seq'}, use_global_device_ids=true, to_apply=%add | all-reduce | flops 128 | bytes 512
  143.6 2.3 reduce-window.16
  146.3 1.8 copy.44
  148.1 2.4 reshape.99
  150.5 6.7 %all-gather.5.cloned.1.call-done = bf16[128,64,128]{2,1,0:T(8,128)(2,1)} async-done(((bf16[8,64,128]{2,1,0:T(8,128)(2,1)}), bf16[128,64,128]{2,1,0:T(8,128)(2,1)}) %all-gather.5.cloned.1.call-update) | async-done | bytes 2097168 | tf_op jit(solution)/shard_map/all_gather | solution.py:21
  157.2 16.9 %while.28 = (s32[]{:T(128)}, f32[8,64,128]{2,1,0:T(8,128)S(1)}, s32[]{:T(128)}, bf16[16,8]{1,0:T(8,128)(2,1)S(1)}, bf16[16,8,64,128]{3,2,1,0:T(8,128)(2,1)}, /*index=5*/s32[]{:T(128)}, s32[]{:T(128)}) while((s32[]{:T(128)}, f32[8,64,128]{2,1,0:T(8,128)S(1)}, s32[]{:T(128)}, bf16[16,8]{1,0:T(8,128)(2,1)S(1)}, ...), condition=%wide.region_6.7_spmd.clone, body=%wide.region_5.6_spmd.clone.sunk | while | flops 327692 | bytes 655545 | solution.py:34
  157.2 1.0 fusion.101
  158.3 1.0 fusion.101
  159.3 1.0 fusion.101
  160.4 1.0 fusion.101
  161.4 1.0 fusion.101
  162.5 1.0 fusion.101
  163.5 1.0 fusion.101
  164.6 1.0 fusion.101
  165.7 1.0 fusion.101
  166.7 1.0 fusion.101
  167.8 1.0 fusion.101
  168.8 1.0 fusion.101
  169.9 1.0 fusion.101
  170.9 1.0 fusion.101
  172.0 1.0 fusion.101
  173.0 1.0 fusion.101
  174.1 1.0 fusion.65
  175.7 2.1 multiply_add_fusion
  177.8 1.9 copy.45
  179.7 2.0 multiply_reduce_fusion
  181.6 23.6 %all-gather.2 = f32[16384]{0:T(1024)S(1)} all-gather(f32[1024]{0:T(1024)S(1)} %multiply_reduce_fusion), channel_id=4, replica_groups=mesh['seq'=16,'head'=16] {'head'}, dimensions={0}, use_global_device_ids=true | all-gather | bytes 69632 | tf_op jit(solution)/shard_map/all_gather | solution.py:118
  205.3 10.7 %convolution_convert_fusion = bf16[1024,4096]{1,0:T(8,128)(2,1)} fusion(bf16[512,4096]{1,0:T(8,128)(2,1)} %param.25, f32[512]{0:T(512)S(1)} %copy-done.4, f32[1024]{0:T(1024)S(1)} %add_rsqrt_fusion, f32[1024,512]{1,0:T(8,128)S(1)} %copy.45, bf16[1024,512]{1,0:T(8,128)(2,1)} %param.16), kind=kOutput, calls=%fused_computation.51 | convolution fusion | flops 4303880192 | bytes 15734784 | tf_op jit(solution)/shard_map/dot_general | solution.py:123
  216.0 87.6 %reduce-scatter.2.cloned.1.call-done = bf16[64,4096]{1,0:T(8,128)(2,1)} async-done(((bf16[1024,4096]{1,0:T(8,128)(2,1)}), bf16[64,4096]{1,0:T(8,128)(2,1)}) %reduce-scatter.2.cloned.1.call-update) | async-done | bytes 524304 | tf_op jit(solution)/shard_map/reduce_scatter | solution.py:122
  (99 shorter events, 10.6 us)
Async XLA Ops:
  6.5 12.1 %copy-start.2 = (bf16[1024,512]{1,0:T(8,128)(2,1)S(1)}, bf16[1024,512]{1,0:T(8,128)(2,1)}, u32[]{:S(2)}) copy-start(bf16[1024,512]{1,0:T(8,128)(2,1)} %param.15) | copy-start | bytes 3145732
  6.5 150.7 %all-gather.5.cloned.1.call-start = ((), (), s32[]{:S(2)}) async-start(), calls=%async_computation.2 | async-start | bytes 2228224 | tf_op jit(solution)/shard_map/all_gather | solution.py:21
  8.7 11.6 %collective-permute-start.1 = (bf16[3,256]{1,0:T(4,128)(2,1)S(1)}, bf16[3,256]{1,0:T(4,128)(2,1)S(1)}, u32[]{:S(2)}, u32[]{:S(2)}) collective-permute-start(bf16[3,256]{1,0:T(4,128)(2,1)S(1)} %slice.98), channel_id=1, source_target_pairs={{0,16},{16,32},{32,48},{48,64},{64,80},{80,96},{96,112},{112,128},... | collective-permute-start | bytes 4616 | tf_op jit(solution)/shard_map/ppermute | solution.py:15
  11.1 10.6 %collective-permute-start = (bf16[3,512]{1,0:T(4,128)(2,1)S(1)}, bf16[3,512]{1,0:T(4,128)(2,1)S(1)}, u32[]{:S(2)}, u32[]{:S(2)}) collective-permute-start(bf16[3,512]{1,0:T(4,128)(2,1)S(1)} %slice.70), channel_id=1, source_target_pairs={{0,16},{16,32},{32,48},{48,64},{64,80},{80,96},{96,112},{112,128},... | collective-permute-start | bytes 9224 | tf_op jit(solution)/shard_map/ppermute | solution.py:15
  20.3 1.6 copy-start
  29.3 86.5 %copy-start.5 = (u32[256]{0:T(256)S(1)}, u32[256]{0:T(256)}, u32[]{:S(2)}) copy-start(u32[256]{0:T(256)} %constant.75) | copy-start | bytes 3076
  115.7 187.8 %reduce-scatter.2.cloned.1.call-start = ((), (), s32[]{:S(2)}) async-start(), calls=%async_computation.1 | async-start | bytes 8912896 | tf_op jit(solution)/shard_map/reduce_scatter | solution.py:122
  174.1 1.6 copy-start.1
  174.1 1.6 copy-start.3
  179.7 25.6 %copy-start.4 = (f32[512]{0:T(512)S(1)}, f32[512]{0:T(512)}, u32[]{:S(2)}) copy-start(f32[512]{0:T(512)} %param.24) | copy-start | bytes 6148
Sparse Core Ops, SparseCore 0:
  115.8 41.3 all-gather.4
  216.1 87.4 reduce-scatter.1
